TPU v7x, 256 devices: a whole 4x4x8 slice. The times are simulated.
256 devices in a mesh: row: 32 (over z, x), layer: 8 (over y, core).
Axes of the slice: x: 4, y: 4, z: 8, core: 2. Of those that a mesh axis runs over, the one named last changes fastest.
Arguments:
- window_points: int32 [2, 32768], P(None, 'row'), may hold values from 0 to 63
- pivot_points: int32 [2, 512], replicated, may hold values from 0 to 63
- window_factor: bfloat16 [32768, 16384], P('row', 'layer'), may hold values from -1.5 to 1.5
- pivot_factor: bfloat16 [512, 16384], P('row', 'layer'), may hold values from -0.0234375 to 0.0234375
- right_sides: bfloat16 [32768, 512], P('row', 'layer'), may hold values from -6 to 6
- pivot_sides: bfloat16 [512, 512], P('row', 'layer'), may hold values from -6 to 6
Outputs:
- panel_factor: float32 [32768, 512], P('row', 'layer')
- eliminated: float32 [32768, 512], P('row', 'layer')
All inputs are finite; a program needn't handle non-finite values.
Results may differ from a plain program's by a relative error of at most 0.0006.
Values may be sent and summed in bfloat16 or wider, within the bound.
No kernel may reach another device: no remote copies, remote signals or barrier semaphores. Data moves between devices by JAX's collectives and lax.ppermute only.
A program may use at most 64 MiB of HBM per device.

v0:
```python
import jax
import jax.numpy as jnp
from jax import lax
from jax.sharding import PartitionSpec as P

nugget_value = 2.0
variance_value = 4.0
length_scale = 4.0


def matern(first_points, second_points):
    first_float = first_points.astype(jnp.float32)
    second_float = second_points.astype(jnp.float32)
    delta_x = first_float[0][:, None] - second_float[0][None, :]
    delta_y = first_float[1][:, None] - second_float[1][None, :]
    scaled = jnp.sqrt(delta_x * delta_x + delta_y * delta_y) * (jnp.sqrt(3.0) / length_scale)
    return variance_value * (1.0 + scaled) * jnp.exp(-scaled)


def solvers(factor):

    def right_solve(matrix):
        return jax.scipy.linalg.solve_triangular(factor, matrix.T, lower=True).T

    def left_solve(matrix):
        return jax.scipy.linalg.solve_triangular(factor, matrix, lower=True)

    return (right_solve, left_solve)


def shards(window_points, pivot_points, window_factor, pivot_factor, right_sides, pivot_sides):
    pivots, pivot_block = (
        lax.all_gather(pivot_factor, "row", axis=0, tiled=True),
        lax.all_gather(pivot_sides, "row", axis=0, tiled=True),
    )
    contract = (((1,), (1,)), ((), ()))
    partial_value = lax.dot_general(
        window_factor, pivots, contract, preferred_element_type=jnp.float32
    )
    gram_part = lax.dot_general(pivots, pivots, contract, preferred_element_type=jnp.float32)
    count = pivots.shape[0]
    cov_diagonal = matern(pivot_points, pivot_points) + nugget_value * jnp.eye(
        count, dtype=jnp.float32
    )
    layers = lax.axis_size("layer")
    layer_index = lax.axis_index("layer")
    cov_panel = matern(window_points, pivot_points)
    schur_sum, gram_sum = lax.psum((partial_value, gram_part), "layer")
    factor = jnp.linalg.cholesky(cov_diagonal - gram_sum)
    right_solve, left_solve = solvers(factor)
    solved = right_solve(cov_panel - schur_sum)
    reduced = left_solve(pivot_block.astype(jnp.float32))
    eliminated = right_sides.astype(jnp.float32) - jnp.dot(
        solved, reduced, precision=lax.Precision.HIGHEST
    )
    width = count // layers
    panel_out = lax.dynamic_slice_in_dim(solved, layer_index * width, width, 1)
    return (panel_out, eliminated)


def solution(mesh):
    placed = (
        P(None, "row"),
        P(),
        P("row", "layer"),
        P("row", "layer"),
        P("row", "layer"),
        P("row", "layer"),
    )
    return jax.shard_map(
        shards,
        mesh=mesh,
        in_specs=placed,
        out_specs=(P("row", "layer"), P("row", "layer")),
        check_vma=False,
    )
```

profile of v0, /device:TPU:2, one launch (start us, length us, event | category | flops | bytes accessed | tf_op | source)
XLA Modules:
  0.0 346.6 jit_solution(16420953489318087059)
XLA Ops:
  7.2 0.7 all-gather.2.cloned.1.call-update
  7.9 82.2 %all-gather.2.cloned.1.call-done = bf16[512,2048]{1,0:T(8,128)(2,1)} async-done(((bf16[16,2048]{1,0:T(8,128)(2,1)}), bf16[512,2048]{1,0:T(8,128)(2,1)}) %all-gather.2.cloned.1.call-update) | async-done | bytes 2097168 | tf_op jit(solution)/shard_map/all_gather | solution.py:33
  90.2 4.6 %fusion.63 = f32[512,512]{0,1:T(8,128)} fusion(bf16[512,2048]{1,0:T(8,128)(2,1)} %all-gather.2.cloned.1.call-done), kind=kOutput, calls=%fused_computation.104 | convolution fusion | flops 1073741824 | bytes 3145728 | tf_op jit(solution)/shard_map/dot_general | solution.py:40
  94.8 3.7 %fusion.64 = f32[1024,512]{1,0:T(8,128)} fusion(bf16[1024,2048]{1,0:T(8,128)(2,1)S(1)} %copy-done.4, bf16[512,2048]{1,0:T(8,128)(2,1)S(1)} %copy-done.5), kind=kOutput, calls=%fused_computation.105 | convolution fusion | flops 2147483648 | bytes 8388608 | tf_op jit(solution)/shard_map/dot_general | solution.py:37
  98.5 0.6 copy-done.3
  99.2 42.2 %all_gather.7 = bf16[512,64]{1,0:T(8,128)(2,1)S(1)} all-gather(bf16[16,64]{1,0:T(8,128)(2,1)S(1)} %copy-done.2), channel_id=1, replica_groups=mesh['row'=32,'layer'=8] {'row'}, dimensions={0}, use_global_device_ids=true | all-gather | bytes 67584 | tf_op jit(solution)/shard_map/all_gather | solution.py:34
  141.4 0.5 iota_multiply_fusion
  141.9 29.5 %all-reduce.4.cloned.1.call-done = (f32[1024,512]{1,0:T(8,128)}, f32[512,512]{0,1:T(8,128)}) async-done(((f32[1024,512]{1,0:T(8,128)}, f32[512,512]{0,1:T(8,128)}), (f32[1024,512]{1,0:T(8,128)}, f32[512,512]{0,1:T(8,128)})) %all-reduce.4.cloned.1.call-update) | async-done | bytes 3145744 | tf_op jit(solution)/shard_map/psum | solution.py:48
  171.5 2.1 add_subtract_fusion
  173.9 0.9 fusion.12
  174.8 11.7 %cholesky.103 = f32[128,128]{1,0:T(8,128)S(1)} custom-call(f32[128,128]{1,0:T(8,128)S(1)} %cholesky.263), custom_call_target="Cholesky" | custom-call | tf_op jit(solution)/shard_map/jit(cholesky)/cholesky | solution.py:49
  186.6 9.8 %custom-call.34 = f32[1,128,128]{1,2,0:T(8,128)S(1)} custom-call(f32[1,128,128]{2,1,0:T(8,128)S(1)} %get-tuple-element.31), custom_call_target="InvertDiagBlocksLowerTriangular" | custom-call | tf_op jit(solution)/shard_map/jit(cholesky)/cholesky | solution.py:49
  197.1 23.5 %cholesky.215 = f32[128,128]{1,0:T(8,128)S(1)} custom-call(f32[128,128]{1,0:T(8,128)S(1)} %cholesky.267), custom_call_target="Cholesky" | custom-call | tf_op jit(solution)/shard_map/jit(cholesky)/cholesky | solution.py:49
  220.9 9.8 %custom-call.35 = f32[1,128,128]{1,2,0:T(8,128)S(1)} custom-call(f32[1,128,128]{2,1,0:T(8,128)S(1)} %get-tuple-element.29), custom_call_target="InvertDiagBlocksLowerTriangular" | custom-call | tf_op jit(solution)/shard_map/jit(cholesky)/cholesky | solution.py:49
  231.2 0.6 convolution_subtract_fusion.4
  231.8 11.7 %cholesky.236 = f32[128,128]{1,0:T(8,128)S(1)} custom-call(f32[128,128]{1,0:T(8,128)S(1)} %cholesky.272), custom_call_target="Cholesky" | custom-call | tf_op jit(solution)/shard_map/jit(cholesky)/cholesky | solution.py:49
  243.7 9.8 %custom-call.36 = f32[1,128,128]{1,2,0:T(8,128)S(1)} custom-call(f32[1,128,128]{2,1,0:T(8,128)S(1)} %get-tuple-element.27), custom_call_target="InvertDiagBlocksLowerTriangular" | custom-call | tf_op jit(solution)/shard_map/jit(cholesky)/cholesky | solution.py:49
  253.8 0.5 convolution_subtract_fusion.8
  254.3 11.7 %cholesky.253 = f32[128,128]{1,0:T(8,128)S(1)} custom-call(f32[128,128]{1,0:T(8,128)S(1)} %convolution_subtract_fusion.8), custom_call_target="Cholesky" | custom-call | tf_op jit(solution)/shard_map/jit(cholesky)/cholesky | solution.py:49
  266.2 0.6 compare_reduce_fusion.1
  266.8 0.7 compare_reduce_fusion
  267.5 0.6 compare_reduce_fusion.2
  270.6 0.6 triangular_solve.127
  271.3 10.7 %while.1 = (s32[]{:T(128)}, f32[512,512]{0,1:T(8,128)S(1)}, s32[4,2]{0,1:T(2,128)S(1)}, f32[4,128,128]{2,1,0:T(8,128)}, s32[]{:T(128)}) while((s32[]{:T(128)}, f32[512,512]{0,1:T(8,128)S(1)}, s32[4,2]{0,1:T(2,128)S(1)}, f32[4,128,128]{2,1,0:T(8,128)}, s32[]{:T(128)}) %tuple.30), condition=%wide.while_cond, body=%wide.while_body.sunk | while | flops 2 | bytes 393829 | solution.py:23
  271.3 0.5 fusion.79
  271.9 1.3 dynamic-slice.12
  273.3 0.6 bitcast_dynamic-update-slice_fusion.2
  274.0 0.5 fusion.79
  274.5 1.3 dynamic-slice.12
  276.0 0.6 bitcast_dynamic-update-slice_fusion.2
  276.7 0.5 fusion.79
  277.2 1.3 dynamic-slice.12
  278.6 0.6 bitcast_dynamic-update-slice_fusion.2
  279.3 0.5 fusion.79
  279.9 1.3 dynamic-slice.12
  281.3 0.6 bitcast_dynamic-update-slice_fusion.2
  282.0 40.3 %custom-call.37 = f32[4,128,128]{1,2,0:T(8,128)S(1)} custom-call(f32[4,128,128]{2,1,0:T(8,128)} %get-tuple-element.9), custom_call_target="InvertDiagBlocksLowerTriangular" | custom-call | tf_op jit(solution)/shard_map/jit(_solve_triangular)/triangular_solve | solution.py:23
  324.5 3.0 subtract_bitcast_fusion
  327.5 0.6 fusion.13
  328.2 1.0 convolution_subtract_fusion.1
  329.2 0.6 fusion.47
  329.8 1.8 convolution_subtract_fusion
  331.7 0.6 fusion.49
  332.3 2.7 fusion.6
  335.1 0.6 fusion.51
  336.0 0.6 copy-done.6
  336.6 2.2 convolution_subtract_fusion.2
  338.8 0.7 dynamic-slice_bitcast_fusion
  (60 shorter events, 5.8 us)
Async XLA Ops:
  7.2 83.0 %all-gather.2.cloned.1.call-start = ((), (), s32[]{:S(2)}) async-start(), calls=%async_computation | async-start | bytes 2162688 | tf_op jit(solution)/shard_map/all_gather | solution.py:33
  7.9 163.6 %all-reduce.4.cloned.1.call-start = ((), (), s32[]{:S(2)}) async-start(), calls=%async_computation.1 | async-start | bytes 6291456 | tf_op jit(solution)/shard_map/psum | solution.py:48
  90.2 4.6 %copy-start.4 = (bf16[1024,2048]{1,0:T(8,128)(2,1)S(1)}, bf16[1024,2048]{1,0:T(8,128)(2,1)}, u32[]{:S(2)}) copy-start(bf16[1024,2048]{1,0:T(8,128)(2,1)} %param.8) | copy-start | bytes 12582916
  90.2 4.6 %copy-start.5 = (bf16[512,2048]{1,0:T(8,128)(2,1)S(1)}, bf16[512,2048]{1,0:T(8,128)(2,1)}, u32[]{:S(2)}) copy-start(bf16[512,2048]{1,0:T(8,128)(2,1)} %all-gather.2.cloned.1.call-done) | copy-start | bytes 6291460
  98.5 0.7 copy-start.3
  98.5 0.7 copy-start.2
  98.5 42.9 %copy-start.1 = (s32[2,1024]{1,0:T(2,128)S(1)}, s32[2,1024]{1,0:T(2,128)}, u32[]{:S(2)}) copy-start(s32[2,1024]{1,0:T(2,128)} %param.6) | copy-start | bytes 24580
  171.5 2.4 copy-start
  335.7 0.9 copy-start.6
Sparse Core Ops, SparseCore 0:
  10.6 79.5 all-gather.1
  98.6 72.8 all-reduce.3
where the time goes:
time: 350 us; the launch traced here: 347 us
  other arithmetic  137 us (39%)
  waiting for transfers between devices  112 us (32%)
  blocking collectives  42.2 us (12%)
  matrix products  23.1 us (7%)
  between operations  17 us (5%)
  local copies, waits for them, and re-layouts  14.3 us (4%)
    another operation x14, other arithmetic, shards(): factor = jnp.linalg.cholesky(cov_diagonal - gram_sum)  90.2 us
    all_gather x1, waiting for transfers between devices, shards(): lax.all_gather(pivot_factor, 'row', axis=0, tiled=True)  82.2 us
    all_gather x1, blocking collectives, shards(): lax.all_gather(pivot_sides, 'row', axis=0, tiled=True)  42.2 us
    another operation x4, other arithmetic, right_solve(): return jax.scipy.linalg.solve_triangular(factor, matrix.T, lower=True).T  41.2 us
    psum x1, waiting for transfers between devices, shards(): schur_sum, gram_sum = lax.psum((partial_value, gram_part), 'layer')  29.5 us
    another operation x20, local copies, waits for them, and re-layouts  10.6 us
    another operation x7, matrix products, right_solve(): return jax.scipy.linalg.solve_triangular(factor, matrix.T, lower=True).T  8.15 us
  transfers between devices with their start and end apart: 2, of which 2 were waited for; matrix products, arithmetic and copies ran while one was open for 0% of the time, Pallas kernels for 0%

commit v1 on v0

--- a/solution.py
+++ b/solution.py
@@ -6,6 +6,11 @@
 nugget_value = 2.0
 variance_value = 4.0
 length_scale = 4.0
+
+
+def gather_over(x, axis, dim):
+    stack = jnp.stack([x] * lax.axis_size(axis))
+    return jnp.concatenate(lax.all_to_all(stack, axis, 0, 0), axis=dim)
 
 
 def matern(first_points, second_points):
@@ -31,7 +36,7 @@
 def shards(window_points, pivot_points, window_factor, pivot_factor, right_sides, pivot_sides):
     pivots, pivot_block = (
         lax.all_gather(pivot_factor, "row", axis=0, tiled=True),
-        lax.all_gather(pivot_sides, "row", axis=0, tiled=True),
+        gather_over(pivot_sides, "row", 0),
     )
     contract = (((1,), (1,)), ((), ()))
     partial_value = lax.dot_general(

time: 350 us -> 349 us (level)
  blocking collectives: 42.2 us -> 0 us
  waiting for transfers between devices: 112 us -> 147 us
  starting transfers between devices: 0.08 us -> 7.77 us
    all_gather x1 -> x0, blocking collectives: 42.2 us -> none  [shards(): lax.all_gather(pivot_sides, 'row', axis=0, tiled=True)]
    psum x1, waiting for transfers between devices: 29.5 us -> 55.4 us  [shards(): schur_sum, gram_sum = lax.psum((partial_value, gram_part), 'layer')]
    all_to_all x0 -> x1, waiting for transfers between devices: none -> 8.22 us  [gather_over(): return jnp.concatenate(lax.all_to_all(stack, axis, 0, 0), axis=dim)]
    all_to_all x0 -> x1, starting transfers between devices: none -> 7.7 us  [gather_over(): return jnp.concatenate(lax.all_to_all(stack, axis, 0, 0), axis=dim)]
    another operation x20 -> x24, local copies, waits for them, and re-layouts: 10.6 us -> 10.5 us
  transfers between devices with their start and end apart: 2 -> 3, of which waited for: 2 -> 3; matrix products, arithmetic and copies ran while one was open for 0% -> 0% of each run, Pallas kernels for 0% -> 0%
where the time goes in v1:
time: 349 us; the launch traced here: 346 us
  waiting for transfers between devices  147 us (42%)
  other arithmetic  137 us (39%)
  matrix products  23.1 us (7%)
  between operations  17.1 us (5%)
  local copies, waits for them, and re-layouts  14.5 us (4%)
  starting transfers between devices  7.77 us (2%)
    another operation x14, other arithmetic, shards(): factor = jnp.linalg.cholesky(cov_diagonal - gram_sum)  89.9 us
    all_gather x1, waiting for transfers between devices, shards(): lax.all_gather(pivot_factor, 'row', axis=0, tiled=True)  82.3 us
    psum x1, waiting for transfers between devices, shards(): schur_sum, gram_sum = lax.psum((partial_value, gram_part), 'layer')  55.4 us
    another operation x4, other arithmetic, right_solve(): return jax.scipy.linalg.solve_triangular(factor, matrix.T, lower=True).T  40.7 us
    another operation x20, local copies, waits for them, and re-layouts  10.5 us
    all_to_all x1, waiting for transfers between devices, gather_over(): return jnp.concatenate(lax.all_to_all(stack, axis, 0, 0), axis=dim)  8.22 us
    another operation x7, matrix products, right_solve(): return jax.scipy.linalg.solve_triangular(factor, matrix.T, lower=True).T  8.18 us
    all_to_all x1, starting transfers between devices, gather_over(): return jnp.concatenate(lax.all_to_all(stack, axis, 0, 0), axis=dim)  7.7 us
  transfers between devices with their start and end apart: 3, of which 3 were waited for; matrix products, arithmetic and copies ran while one was open for 0% of the time, Pallas kernels for 0%

profile of v1, /device:TPU:2, one launch (start us, length us, event | category | flops | bytes accessed | tf_op | source)
XLA Modules:
  0.0 345.7 jit_solution(3637526151288092265)
XLA Ops:
  7.2 0.7 all-gather.2.cloned.1.call-update
  7.9 82.3 %all-gather.2.cloned.1.call-done = bf16[512,2048]{1,0:T(8,128)(2,1)} async-done(((bf16[16,2048]{1,0:T(8,128)(2,1)}), bf16[512,2048]{1,0:T(8,128)(2,1)}) %all-gather.2.cloned.1.call-update) | async-done | bytes 2097168 | tf_op jit(solution)/shard_map/all_gather | solution.py:38
  90.2 4.6 %fusion.63 = f32[512,512]{0,1:T(8,128)} fusion(bf16[512,2048]{1,0:T(8,128)(2,1)} %all-gather.2.cloned.1.call-done), kind=kOutput, calls=%fused_computation.104 | convolution fusion | flops 1073741824 | bytes 3145728 | tf_op jit(solution)/shard_map/dot_general | solution.py:45
  94.8 3.7 %fusion.64 = f32[1024,512]{1,0:T(8,128)} fusion(bf16[1024,2048]{1,0:T(8,128)(2,1)S(1)} %copy-done.5, bf16[512,2048]{1,0:T(8,128)(2,1)S(1)} %copy-done.6), kind=kOutput, calls=%fused_computation.105 | convolution fusion | flops 2147483648 | bytes 8388608 | tf_op jit(solution)/shard_map/dot_general | solution.py:42
  98.5 0.7 copy-done.3
  99.2 0.8 reshape.86
  100.0 7.7 %all-to-all-start = ((bf16[32,2,512]{2,1,0:T(2,128)(2,1)}), bf16[32,2,512]{2,1,0:T(2,128)(2,1)S(1)}, u32[]{:S(2)}, u32[]{:S(2)}) async-start(bf16[32,2,512]{2,1,0:T(2,128)(2,1)} %reshape.86), calls=%async_computation | async-start | bytes 131072 | tf_op jit(solution)/shard_map/all_to_all | solution.py:13
  107.8 8.2 %all-to-all-done = bf16[32,2,512]{2,1,0:T(2,128)(2,1)S(1)} async-done(((bf16[32,2,512]{2,1,0:T(2,128)(2,1)}), bf16[32,2,512]{2,1,0:T(2,128)(2,1)S(1)}, u32[]{:S(2)}, u32[]{:S(2)}) %all-to-all-start) | async-done | bytes 65568 | tf_op jit(solution)/shard_map/all_to_all | solution.py:13
  116.2 55.4 %all-reduce.4.cloned.1.call-done = (f32[1024,512]{1,0:T(8,128)}, f32[512,512]{0,1:T(8,128)}) async-done(((f32[1024,512]{1,0:T(8,128)}, f32[512,512]{0,1:T(8,128)}), (f32[1024,512]{1,0:T(8,128)}, f32[512,512]{0,1:T(8,128)})) %all-reduce.4.cloned.1.call-update) | async-done | bytes 3145744 | tf_op jit(solution)/shard_map/psum | solution.py:53
  171.6 2.1 add_subtract_fusion
  174.0 0.9 fusion.12
  174.9 11.7 %cholesky.103 = f32[128,128]{1,0:T(8,128)S(1)} custom-call(f32[128,128]{1,0:T(8,128)S(1)} %cholesky.263), custom_call_target="Cholesky" | custom-call | tf_op jit(solution)/shard_map/jit(cholesky)/cholesky | solution.py:54
  186.7 9.8 %custom-call.34 = f32[1,128,128]{1,2,0:T(8,128)S(1)} custom-call(f32[1,128,128]{2,1,0:T(8,128)S(1)} %get-tuple-element.34), custom_call_target="InvertDiagBlocksLowerTriangular" | custom-call | tf_op jit(solution)/shard_map/jit(cholesky)/cholesky | solution.py:54
  197.2 23.3 %cholesky.215 = f32[128,128]{1,0:T(8,128)S(1)} custom-call(f32[128,128]{1,0:T(8,128)S(1)} %cholesky.267), custom_call_target="Cholesky" | custom-call | tf_op jit(solution)/shard_map/jit(cholesky)/cholesky | solution.py:54
  220.8 9.8 %custom-call.35 = f32[1,128,128]{1,2,0:T(8,128)S(1)} custom-call(f32[1,128,128]{2,1,0:T(8,128)S(1)} %get-tuple-element.32), custom_call_target="InvertDiagBlocksLowerTriangular" | custom-call | tf_op jit(solution)/shard_map/jit(cholesky)/cholesky | solution.py:54
  231.1 0.6 convolution_subtract_fusion.4
  231.7 11.7 %cholesky.236 = f32[128,128]{1,0:T(8,128)S(1)} custom-call(f32[128,128]{1,0:T(8,128)S(1)} %cholesky.272), custom_call_target="Cholesky" | custom-call | tf_op jit(solution)/shard_map/jit(cholesky)/cholesky | solution.py:54
  243.6 9.8 %custom-call.36 = f32[1,128,128]{1,2,0:T(8,128)S(1)} custom-call(f32[1,128,128]{2,1,0:T(8,128)S(1)} %get-tuple-element.30), custom_call_target="InvertDiagBlocksLowerTriangular" | custom-call | tf_op jit(solution)/shard_map/jit(cholesky)/cholesky | solution.py:54
  253.7 0.5 convolution_subtract_fusion.8
  254.2 11.7 %cholesky.253 = f32[128,128]{1,0:T(8,128)S(1)} custom-call(f32[128,128]{1,0:T(8,128)S(1)} %convolution_subtract_fusion.8), custom_call_target="Cholesky" | custom-call | tf_op jit(solution)/shard_map/jit(cholesky)/cholesky | solution.py:54
  266.0 0.6 compare_reduce_fusion.1
  266.6 0.7 compare_reduce_fusion
  267.3 0.6 compare_reduce_fusion.2
  270.5 10.6 %while.1 = (s32[]{:T(128)}, f32[512,512]{0,1:T(8,128)S(1)}, s32[4,2]{0,1:T(2,128)S(1)}, f32[4,128,128]{2,1,0:T(8,128)}, s32[]{:T(128)}) while((s32[]{:T(128)}, f32[512,512]{0,1:T(8,128)S(1)}, s32[4,2]{0,1:T(2,128)S(1)}, f32[4,128,128]{2,1,0:T(8,128)}, s32[]{:T(128)}) %tuple.32), condition=%wide.while_cond, body=%wide.while_body.sunk | while | flops 2 | bytes 393829 | solution.py:28
  270.6 0.6 fusion.80
  271.1 1.3 dynamic-slice.12
  272.5 0.6 bitcast_dynamic-update-slice_fusion.2
  273.2 0.6 fusion.80
  273.8 1.3 dynamic-slice.12
  275.1 0.6 bitcast_dynamic-update-slice_fusion.2
  275.9 0.6 fusion.80
  276.4 1.3 dynamic-slice.12
  277.8 0.6 bitcast_dynamic-update-slice_fusion.2
  278.5 0.6 fusion.80
  279.1 1.3 dynamic-slice.12
  280.4 0.6 bitcast_dynamic-update-slice_fusion.2
  281.1 40.3 %custom-call.37 = f32[4,128,128]{1,2,0:T(8,128)S(1)} custom-call(f32[4,128,128]{2,1,0:T(8,128)} %get-tuple-element.9), custom_call_target="InvertDiagBlocksLowerTriangular" | custom-call | tf_op jit(solution)/shard_map/jit(_solve_triangular)/triangular_solve | solution.py:28
  323.6 3.0 subtract_bitcast_fusion
  326.6 0.7 fusion.13
  327.3 1.0 convolution_subtract_fusion.1
  328.3 0.6 fusion.47
  328.9 1.8 convolution_subtract_fusion
  330.8 0.6 fusion.49
  331.4 2.8 fusion.6
  334.2 0.6 fusion.51
  335.1 0.6 copy-done.7
  335.8 2.2 convolution_subtract_fusion.2
  337.9 0.7 dynamic-slice_bitcast_fusion
  (68 shorter events, 5.9 us)
Async XLA Ops:
  7.2 83.0 %all-gather.2.cloned.1.call-start = ((), (), s32[]{:S(2)}) async-start(), calls=%async_computation.1 | async-start | bytes 2162688 | tf_op jit(solution)/shard_map/all_gather | solution.py:38
  7.9 163.7 %all-reduce.4.cloned.1.call-start = ((), (), s32[]{:S(2)}) async-start(), calls=%async_computation.2 | async-start | bytes 6291456 | tf_op jit(solution)/shard_map/psum | solution.py:53
  90.2 4.6 %copy-start.5 = (bf16[1024,2048]{1,0:T(8,128)(2,1)S(1)}, bf16[1024,2048]{1,0:T(8,128)(2,1)}, u32[]{:S(2)}) copy-start(bf16[1024,2048]{1,0:T(8,128)(2,1)} %param.8) | copy-start | bytes 12582916
  90.2 4.6 %copy-start.6 = (bf16[512,2048]{1,0:T(8,128)(2,1)S(1)}, bf16[512,2048]{1,0:T(8,128)(2,1)}, u32[]{:S(2)}) copy-start(bf16[512,2048]{1,0:T(8,128)(2,1)} %all-gather.2.cloned.1.call-done) | copy-start | bytes 6291460
  98.5 0.7 copy-start.3
  98.5 9.2 %copy-start.4 = (s32[2,512]{1,0:T(2,128)S(1)}, s32[2,512]{1,0:T(2,128)}, u32[]{:S(2)}) copy-start(s32[2,512]{1,0:T(2,128)} %param.7) | copy-start | bytes 12292
  98.5 9.2 %copy-start.2 = (s32[2,1024]{1,0:T(2,128)S(1)}, s32[2,1024]{1,0:T(2,128)}, u32[]{:S(2)}) copy-start(s32[2,1024]{1,0:T(2,128)} %param.6) | copy-start | bytes 24580
  100.0 16.0 %all-to-all-start = ((bf16[32,2,512]{2,1,0:T(2,128)(2,1)}), bf16[32,2,512]{2,1,0:T(2,128)(2,1)S(1)}, u32[]{:S(2)}, u32[]{:S(2)}) async-start(bf16[32,2,512]{2,1,0:T(2,128)(2,1)} %reshape.86), calls=%async_computation | async-start | bytes 131072 | tf_op jit(solution)/shard_map/all_to_all | solution.py:13
  116.2 57.9 %copy-start.1 = (bf16[32,16,64]{2,1,0:T(8,128)(2,1)}, bf16[32,16,64]{2,1,0:T(8,128)(2,1)S(1)}, u32[]{:S(2)}) copy-start(bf16[32,16,64]{2,1,0:T(8,128)(2,1)S(1)} %reshape.87) | copy-start | bytes 196612
  171.6 2.5 copy-start
  270.3 51.0 %slice-start = ((bf16[32,16,64]{2,1,0:T(8,128)(2,1)}), bf16[8,16,64]{2,1,0:T(8,128)(2,1)S(1)}, s32[]{:S(2)}) async-start(bf16[32,16,64]{2,1,0:T(8,128)(2,1)} %copy-done.1), calls=%async_computation.3 | async-start | bytes 65536 | tf_op jit(solution)/shard_map/jit(_solve_triangular)/triangular_solve | solution.py:31
  334.9 0.9 copy-start.7
Sparse Core Ops, SparseCore 0:
  10.6 79.6 all-gather.1
  98.7 72.8 all-reduce.3
